TPU v7x, 512 devices: a whole 4x4x16 slice. The times are simulated.
512 devices in a mesh: dp: 32 (over z, core), table: 16 (over x, y).
Axes of the slice: x: 4, y: 4, z: 16, core: 2. Of those that a mesh axis runs over, the one named last changes fastest.
Arguments:
- node_table: bfloat16 [1048576, 256], P(('dp', 'table')), may hold values from -6 to 6
- user_vectors: bfloat16 [131072, 256], P(('dp', 'table')), may hold values from -6 to 6
- first_weight: bfloat16 [768, 256], replicated, may hold values from -0.21875 to 0.21875
- first_bias: float32 [256], replicated, may hold values from -3 to 3
- second_weight: bfloat16 [256, 128], replicated, may hold values from -0.375 to 0.375
- second_bias: float32 [128], replicated, may hold values from -3 to 3
- out_weight: bfloat16 [128], replicated, may hold values from -0.5 to 0.5
- panel_rows: int32 [512, 512, 4], P(('dp', 'table')), may hold values from -1 to 2047, as said below
- pair_slots: int32 [131072, 8], P(('dp', 'table')), may hold values from 0 to 2047, as said below
Outputs:
- grad_table: float32 [1048576, 256], P(('dp', 'table'))
- grad_users: bfloat16 [131072, 256], P(('dp', 'table'))
Inputs may be any that keep to these rules, and one draw needn't show every extreme that they name: panel_rows[d, o, j] is a row among owner o's 2048 rows (node o * 2048 + row) that device d's users visit, or -1 for an unused slot; the used slots of each d and o come first, 1 to 4 of them; every device uses all 4 slots on some owner, and some owners, the last one among them, have all 4 slots used by every device. pair_slots[u, k] = o * 4 + j names a used slot j of owner o in panel_rows[d, o] of the user's device d = u // 256; column 0 is the user's positive node, the others its beam negatives.
All inputs are finite; a program needn't handle non-finite values.
Results may differ from a plain program's by a relative error of at most 0.0052.
Values may be sent and summed in bfloat16 or wider, within the bound.
No kernel may reach another device: no remote copies, remote signals or barrier semaphores. Data moves between devices by JAX's collectives and lax.ppermute only.
A program may use at most 64 MiB of HBM per device.

v0:
```python
import jax
import jax.numpy as jnp
from jax import lax
from jax.sharding import PartitionSpec as P

loss_scale = 32.0


def silu_slope(value):
    sig = jax.nn.sigmoid(value)
    return sig * (1.0 + value * (1.0 - sig))


def body(
    node_table,
    user_vectors,
    first_weight,
    first_bias,
    second_weight,
    second_bias,
    out_weight,
    panel_rows,
    pair_slots,
):
    count_dp = lax.axis_size("dp")
    count_table = lax.axis_size("table")
    own_rows, feat_width = node_table.shape
    slot_cap = panel_rows.shape[2]
    wanted = panel_rows.reshape(count_dp, count_table, slot_cap)
    requested = lax.all_to_all(
        lax.all_to_all(wanted, "dp", split_axis=0, concat_axis=0, tiled=True),
        "table",
        split_axis=1,
        concat_axis=1,
        tiled=True,
    )
    flat_requested = requested.reshape(-1)
    safe_rows = jnp.maximum(flat_requested, 0)
    picked = jnp.take(node_table, safe_rows, axis=0)
    picked = jnp.where((flat_requested >= 0)[:, None], picked, jnp.zeros_like(picked))
    picked = picked.reshape(count_dp, count_table, slot_cap, feat_width)
    panels = lax.all_to_all(
        lax.all_to_all(picked, "dp", split_axis=0, concat_axis=0, tiled=True),
        "table",
        split_axis=1,
        concat_axis=1,
        tiled=True,
    )
    panels = panels.reshape(count_dp * count_table * slot_cap, feat_width)
    user_count, per_user = pair_slots.shape
    block_users = min(256, user_count)
    block_total = user_count // block_users
    weight_user = first_weight[:feat_width]
    weight_item = first_weight[feat_width : 2 * feat_width]
    weight_cross = first_weight[2 * feat_width :]
    out_f32 = out_weight.astype(jnp.float32)

    def run_block(block_data):
        user_block, slot_block = block_data
        item_vecs = jnp.take(panels, slot_block.reshape(-1), axis=0)
        item_three = item_vecs.reshape(block_users, per_user, feat_width)
        user_f32 = user_block.astype(jnp.float32)[:, None, :]
        item_f32 = item_three.astype(jnp.float32)
        crossed = (user_f32 * item_f32).astype(jnp.bfloat16).reshape(-1, feat_width)
        user_part = jnp.dot(user_block, weight_user, preferred_element_type=jnp.float32)
        pair_part = jnp.dot(item_vecs, weight_item, preferred_element_type=jnp.float32) + jnp.dot(
            crossed, weight_cross, preferred_element_type=jnp.float32
        )
        pre_first = (
            pair_part.reshape(block_users, per_user, -1) + user_part[:, None, :] + first_bias
        ).reshape(block_users * per_user, -1)
        hid_first = jax.nn.silu(pre_first).astype(jnp.bfloat16)
        pre_second = (
            jnp.dot(hid_first, second_weight, preferred_element_type=jnp.float32) + second_bias
        )
        hid_second = jax.nn.silu(pre_second).astype(jnp.bfloat16)
        logits = jnp.dot(hid_second, out_weight, preferred_element_type=jnp.float32)
        targets = (
            (lax.broadcasted_iota(jnp.int32, (block_users, per_user), 1) == 0)
            .astype(jnp.float32)
            .reshape(-1)
        )
        logit_grad = loss_scale * (jax.nn.sigmoid(logits) - targets)
        delta_second = (logit_grad[:, None] * out_f32[None, :] * silu_slope(pre_second)).astype(
            jnp.bfloat16
        )
        delta_first = (
            jnp.dot(delta_second, second_weight.T, preferred_element_type=jnp.float32)
            * silu_slope(pre_first)
        ).astype(jnp.bfloat16)
        backward = jnp.dot(delta_first, first_weight.T, preferred_element_type=jnp.float32)
        backward = backward.reshape(block_users, per_user, 3 * feat_width)
        grad_items = (
            backward[:, :, feat_width : 2 * feat_width]
            + backward[:, :, 2 * feat_width :] * user_f32
        )
        grad_users = jnp.sum(
            backward[:, :, :feat_width] + backward[:, :, 2 * feat_width :] * item_f32, axis=1
        ).astype(jnp.bfloat16)
        return (grad_items.reshape(block_users * per_user, feat_width), grad_users)

    item_grads, user_grads = lax.map(
        run_block,
        (
            user_vectors.reshape(block_total, block_users, feat_width),
            pair_slots.reshape(block_total, block_users, per_user),
        ),
    )
    slot_grads = jax.ops.segment_sum(
        item_grads.reshape(-1, feat_width),
        pair_slots.reshape(-1),
        num_segments=count_dp * count_table * slot_cap,
    )
    slot_grads = slot_grads.reshape(count_dp, count_table, slot_cap, feat_width)
    returned = lax.all_to_all(
        lax.all_to_all(
            slot_grads.astype(jnp.bfloat16), "dp", split_axis=0, concat_axis=0, tiled=True
        ),
        "table",
        split_axis=1,
        concat_axis=1,
        tiled=True,
    ).astype(slot_grads.dtype)
    grad_table = jax.ops.segment_sum(
        returned.reshape(-1, feat_width), safe_rows, num_segments=own_rows
    )
    return (grad_table, user_grads.reshape(user_count, feat_width))


def solution(mesh):
    placed = (
        P(("dp", "table"), None),
        P(("dp", "table"), None),
        P(),
        P(),
        P(),
        P(),
        P(),
        P(("dp", "table"), None, None),
        P(("dp", "table"), None),
    )
    return jax.shard_map(
        body,
        mesh=mesh,
        in_specs=placed,
        out_specs=(P(("dp", "table"), None), P(("dp", "table"), None)),
        check_vma=False,
    )
```

profile of v0, /device:TPU:1, one launch (start us, length us, event | category | flops | bytes accessed | tf_op | source)
XLA Modules:
  0.0 277.4 jit_solution(5534415665663142336)
XLA Ops:
  0.6 0.0 copy-start
  0.6 0.9 reshape.95
  1.6 29.5 %all_to_all.30 = s32[32,16,4]{1,2,0:T(4,128)S(1)} all-to-all(s32[32,16,4]{1,2,0:T(4,128)S(1)} %copy.40), channel_id=1, replica_groups=mesh['dp'=32,'table'=16] {'dp'}, dimensions={0} | all-to-all | bytes 16384 | tf_op jit(solution)/shard_map/all_to_all | solution.py:31
  31.1 0.1 copy.41
  31.2 0.1 reshape.153
  31.3 13.0 %all_to_all.31 = s32[16,1,128]{2,1,0:T(1,128)S(1)} all-to-all(s32[16,1,128]{2,1,0:T(1,128)S(1)} %reshape.153), channel_id=1, replica_groups=mesh['dp'=32,'table'=16] {'table'}, dimensions={0} | all-to-all | bytes 16384 | tf_op jit(solution)/shard_map/all_to_all | solution.py:30
  44.3 0.5 broadcast.80
  44.8 0.7 reduce
  45.5 0.1 reshape.154
  45.6 0.2 copy.43
  45.8 0.2 reshape.132
  46.0 0.2 copy.46
  46.2 0.2 ge.16
  46.4 0.0 copy-done
  46.5 7.5 %gather_fusion = bf16[2048,256]{1,0:T(8,128)(2,1)S(1)} fusion(bf16[2048,256]{1,0:T(8,128)(2,1)S(1)} %copy-done, s32[2048]{0:T(1024)S(1)} %fusion.30), kind=kCustom, calls=%fused_computation.clone | custom fusion | bytes 2105344 | tf_op jit(solution)/shard_map/jit(_take)/gather | solution.py:39
  54.0 1.5 select_select_fusion
  55.5 0.3 reshape.96
  55.7 61.5 %all_to_all.32 = bf16[32,16,4,256]{3,2,1,0:T(4,128)(2,1)S(1)} all-to-all(bf16[32,16,4,256]{3,2,1,0:T(4,128)(2,1)S(1)} %reshape.96), channel_id=1, replica_groups=mesh['dp'=32,'table'=16] {'dp'}, dimensions={0} | all-to-all | bytes 2097152 | tf_op jit(solution)/shard_map/all_to_all | solution.py:43
  117.2 0.0 copy-start.9
  117.2 0.0 copy-start.3
  117.2 1.5 copy.47
  118.7 3.7 %all-to-all-start.3 = ((bf16[32,16,4,256]{3,2,0,1:T(4,128)(2,1)}), bf16[32,16,4,256]{3,2,0,1:T(4,128)(2,1)S(1)}, u32[]{:S(2)}, u32[]{:S(2)}) async-start(bf16[32,16,4,256]{3,2,0,1:T(4,128)(2,1)} %copy.47), calls=%async_computation.3 | async-start | bytes 2097152 | tf_op jit(solution)/shard_map/all_to_all | solution.py:42
  122.4 0.0 copy-done.9
  122.4 0.1 convert_element_type.65
  122.5 0.0 copy-done.5
  122.5 0.1 copy.44
  122.7 0.1 reshape.124
  122.8 0.0 copy-done.3
  122.8 1.8 fusion.25
  124.6 13.4 %all-to-all-done.3 = bf16[32,16,4,256]{3,2,0,1:T(4,128)(2,1)S(1)} async-done(((bf16[32,16,4,256]{3,2,0,1:T(4,128)(2,1)}), bf16[32,16,4,256]{3,2,0,1:T(4,128)(2,1)S(1)}, u32[]{:S(2)}, u32[]{:S(2)}) %all-to-all-start.3) | async-done | bytes 1048608 | tf_op jit(solution)/shard_map/all_to_all | solution.py:42
  138.0 1.5 copy.48
  139.5 1.3 reshape.97
  140.9 7.5 %gather_fusion.1 = bf16[2048,256]{1,0:T(8,128)(2,1)S(1)} fusion(bf16[2048,256]{1,0:T(8,128)(2,1)S(1)} %reshape.97, s32[2048]{0:T(1024)S(1)} %fusion.31), kind=kCustom, calls=%fused_computation.1.clone | custom fusion | bytes 2105344 | tf_op jit(solution)/shard_map/while/body/eval_jaxpr/jit(_take)/gather | solution.py:60
  148.4 0.0 copy-start.2
  148.4 0.0 copy-start.4
  148.4 0.0 copy-start.6
  148.4 1.5 fusion.28
  149.9 0.0 copy-done.2
  149.9 0.0 copy-done.4
  149.9 0.0 copy-done.6
  149.9 0.0 copy-start.7
  149.9 0.0 copy-start.8
  149.9 0.7 fusion.1
  150.7 0.1 copy-done.7
  150.7 0.0 copy-done.8
  150.7 0.0 copy-start.1
  150.7 0.7 convolution_add_fusion.1
  151.4 0.6 copy-done.1
  152.1 0.0 copy-start.10
  152.1 0.4 fusion.24
  152.5 0.6 copy-done.10
  153.1 6.4 %convolution_bitcast_fusion = f32[256,8,768]{2,1,0:T(8,128)} fusion(bf16[768,256]{1,0:T(8,128)(2,1)S(1)} %copy-done.4, bf16[256,128]{1,0:T(8,128)(2,1)S(1)} %copy-done.7, f32[2048,256]{1,0:T(8,128)} %copy-done.1, f32[2048,128]{1,0:T(8,128)} %copy-done.10, f32[128]{0:T(128)S(1)} %convert_element_type.66, f32[2048]{0:T(1024)S(1)} %subtract_multiply_fusion), kind=kOutput, calls=%fused_computation.8 | convolution fusion | flops 946864128 | bytes 9904640 | tf_op jit(solution)/shard_map/while/body/eval_jaxpr/dot_general | solution.py:91
  159.5 13.8 %scatter_custom_fusion = f32[2048,256]{1,0:T(8,128)} fusion(s32[2048]{0:T(1024)S(1)} %reshape.124, f32[256,8,768]{2,1,0:T(8,128)} %convolution_bitcast_fusion, f32[256,256]{1,0:T(8,128)S(1)} %convert_element_type.59, f32[]{:T(128)} %constant.21.clone.1), kind=kCustom, calls=%fused_computation.19 | custom fusion | flops 1572864 | bytes 6554112 | tf_op jit(solution)/shard_map/scatter-add | solution.py:109
  173.3 1.7 convert_element_type.69
  175.0 1.1 convert_element_type.70
  176.1 62.3 %all_to_all.33 = bf16[32,16,4,256]{3,2,1,0:T(4,128)(2,1)S(1)} all-to-all(bf16[32,16,4,256]{3,2,1,0:T(4,128)(2,1)} %convert_element_type.70), channel_id=1, replica_groups=mesh['dp'=32,'table'=16] {'dp'}, dimensions={0} | all-to-all | bytes 2097152 | tf_op jit(solution)/shard_map/all_to_all | solution.py:116
  238.5 1.5 copy.49
  239.9 3.7 %all-to-all-start.5 = ((bf16[32,16,4,256]{3,2,0,1:T(4,128)(2,1)}), bf16[32,16,4,256]{3,2,0,1:T(4,128)(2,1)S(1)}, u32[]{:S(2)}, u32[]{:S(2)}) async-start(bf16[32,16,4,256]{3,2,0,1:T(4,128)(2,1)} %copy.49), calls=%async_computation.5 | async-start | bytes 2097152 | tf_op jit(solution)/shard_map/all_to_all | solution.py:115
  243.6 3.7 %fusion.6 = bf16[256,256]{1,0:T(8,128)(2,1)} fusion(f32[256,8,768]{2,1,0:T(8,128)} %convolution_bitcast_fusion, bf16[2048,256]{1,0:T(8,128)(2,1)S(1)} %gather_fusion.1, pred[2048]{0:T(1024)(128)(4,1)S(1)} %compare_and_fusion), kind=kLoop, calls=%fused_computation.16 | loop fusion | flops 2555904 | bytes 5376000 | tf_op jit(solution)/shard_map/while/body/eval_jaxpr/reduce_sum | solution.py:97
  247.3 11.9 %all-to-all-done.5 = bf16[32,16,4,256]{3,2,0,1:T(4,128)(2,1)S(1)} async-done(((bf16[32,16,4,256]{3,2,0,1:T(4,128)(2,1)}), bf16[32,16,4,256]{3,2,0,1:T(4,128)(2,1)S(1)}, u32[]{:S(2)}, u32[]{:S(2)}) %all-to-all-start.5) | async-done | bytes 1048608 | tf_op jit(solution)/shard_map/all_to_all | solution.py:115
  259.2 1.2 copy_convert_fusion
  260.5 1.8 copy.51
  262.2 1.8 reshape.134
  264.0 13.4 %scatter_custom_fusion.1 = f32[2048,256]{1,0:T(8,128)} fusion(s32[2048]{0:T(1024)S(1)} %reshape.132, f32[2048,256]{1,0:T(8,128)} %reshape.134, f32[]{:T(128)} %constant.21.clone.1), kind=kCustom, calls=%fused_computation.31 | custom fusion | flops 524288 | bytes 2097664 | tf_op jit(solution)/shard_map/scatter-add | solution.py:124
  (13 shorter events, 0.1 us)
Async XLA Ops:
  0.6 45.8 %copy-start = (bf16[2048,256]{1,0:T(8,128)(2,1)S(1)}, bf16[2048,256]{1,0:T(8,128)(2,1)}, u32[]{:S(2)}) copy-start(bf16[2048,256]{1,0:T(8,128)(2,1)} %param.11) | copy-start | bytes 3145732
  117.2 5.1 %copy-start.9 = (bf16[128]{0:T(256)(128)(2,1)S(1)}, bf16[128]{0:T(256)(128)(2,1)}, u32[]{:S(2)}) copy-start(bf16[128]{0:T(256)(128)(2,1)} %param.17) | copy-start | bytes 772
  117.2 5.3 %copy-start.5 = (s32[256,8]{0,1:T(8,128)S(1)}, s32[256,8]{0,1:T(8,128)}, u32[]{:S(2)}) copy-start(s32[256,8]{0,1:T(8,128)} %param.19) | copy-start | bytes 24580
  117.2 5.6 %copy-start.3 = (bf16[256,256]{1,0:T(8,128)(2,1)S(1)}, bf16[256,256]{1,0:T(8,128)(2,1)}, u32[]{:S(2)}) copy-start(bf16[256,256]{1,0:T(8,128)(2,1)} %param.12) | copy-start | bytes 393220
  118.7 19.3 %all-to-all-start.3 = ((bf16[32,16,4,256]{3,2,0,1:T(4,128)(2,1)}), bf16[32,16,4,256]{3,2,0,1:T(4,128)(2,1)S(1)}, u32[]{:S(2)}, u32[]{:S(2)}) async-start(bf16[32,16,4,256]{3,2,0,1:T(4,128)(2,1)} %copy.47), calls=%async_computation.3 | async-start | bytes 2097152 | tf_op jit(solution)/shard_map/all_to_all | solution.py:42
  148.4 1.5 copy-start.2
  148.4 1.5 copy-start.4
  148.4 1.5 copy-start.6
  149.9 0.8 copy-start.7
  149.9 0.8 copy-start.8
  150.7 1.3 copy-start.1
  152.1 1.0 copy-start.10
  239.9 19.3 %all-to-all-start.5 = ((bf16[32,16,4,256]{3,2,0,1:T(4,128)(2,1)}), bf16[32,16,4,256]{3,2,0,1:T(4,128)(2,1)S(1)}, u32[]{:S(2)}, u32[]{:S(2)}) async-start(bf16[32,16,4,256]{3,2,0,1:T(4,128)(2,1)} %copy.49), calls=%async_computation.5 | async-start | bytes 2097152 | tf_op jit(solution)/shard_map/all_to_all | solution.py:115
where the time goes:
time: 279 us; the launch traced here: 277 us
  blocking collectives  166 us (59%)
  other arithmetic  36.1 us (13%)
  local copies, waits for them, and re-layouts  30 us (11%)
  waiting for transfers between devices  25.3 us (9%)
  matrix products  11.5 us (4%)
  starting transfers between devices  7.31 us (3%)
    all_to_all x1, blocking collectives, body(): lax.all_to_all(slot_grads.astype(jnp.bfloat16), 'dp', split_axis=0, conca...  62.3 us
    all_to_all x1, blocking collectives, body(): lax.all_to_all(picked, 'dp', split_axis=0, concat_axis=0, tiled=True)  61.5 us
    all_to_all x1, blocking collectives, body(): lax.all_to_all(wanted, 'dp', split_axis=0, concat_axis=0, tiled=True)  29.5 us
    scatter-add x1, other arithmetic, body(): jax.ops.segment_sum(item_grads.reshape(-1, feat_width), pair_slots.reshap...  13.8 us
    scatter-add x1, other arithmetic, body(): jax.ops.segment_sum(returned.reshape(-1, feat_width), safe_rows, num_segm...  13.4 us
    all_to_all x1, waiting for transfers between devices, body(): lax.all_to_all(lax.all_to_all(picked, 'dp', split_axis=0, concat_axis=0,...  13.4 us
    all_to_all x1, blocking collectives, body(): lax.all_to_all(lax.all_to_all(wanted, 'dp', split_axis=0, concat_axis=0,...  13 us
    all_to_all x1, waiting for transfers between devices, body(): lax.all_to_all(lax.all_to_all(slot_grads.astype(jnp.bfloat16), 'dp', spli...  11.9 us
  transfers between devices with their start and end apart: 2, of which 2 were waited for; matrix products, arithmetic and copies ran while one was open for 2% of the time, Pallas kernels for 0%

commit v1 on v0

v1 whole, which is shorter than its diff:
```python
import jax
import jax.numpy as jnp
from jax import lax
from jax.experimental import pallas as pl
from jax.experimental.pallas import tpu as pltpu
from jax.sharding import PartitionSpec as P

loss_scale = 32.0
BOTH = ("dp", "table")
ROW_BLOCK = 512


def slope_of(value, sig):
    return sig * (1.0 + value * (1.0 - sig))


def pick_kernel(index_ref, table_ref, out_ref):
    rows = table_ref.shape[0]
    table = table_ref[...]
    columns = index_ref[...].T
    per_block = ROW_BLOCK // 128
    for block in range(out_ref.shape[0] // ROW_BLOCK):
        hot = []
        for part in range(per_block):
            at = block * per_block + part
            wanted = columns[:, at : at + 1]
            hot.append(wanted == lax.broadcasted_iota(jnp.int32, (128, rows), 1))
        hot = jnp.concatenate([one.astype(jnp.float32) for one in hot], axis=0).astype(jnp.bfloat16)
        out_ref[block * ROW_BLOCK : (block + 1) * ROW_BLOCK, :] = jnp.dot(
            hot, table, preferred_element_type=jnp.float32
        ).astype(out_ref.dtype)


def pick_rows(index, table):
    count = index.size
    return pl.pallas_call(
        pick_kernel,
        out_shape=jax.ShapeDtypeStruct((count, table.shape[1]), table.dtype),
        in_specs=[pl.BlockSpec(memory_space=pltpu.VMEM)] * 2,
        out_specs=pl.BlockSpec(memory_space=pltpu.VMEM),
        name="pick_rows",
    )(index.reshape(count // 128, 128), table)


def sum_block(index_row, first, values):
    count = index_row.shape[1]
    row_id = lax.broadcasted_iota(jnp.int32, (ROW_BLOCK, count), 0) + first
    hot = (row_id == index_row).astype(jnp.float32).astype(jnp.bfloat16)
    return jnp.dot(hot, values, preferred_element_type=jnp.float32)


def sum_kernel(index_ref, value_ref, out_ref):
    first = pl.program_id(0) * ROW_BLOCK
    out_ref[...] = sum_block(index_ref[...], first, value_ref[...])


def sum_rows(index_row, values, rows):
    count, width = values.shape
    return pl.pallas_call(
        sum_kernel,
        out_shape=jax.ShapeDtypeStruct((rows, width), jnp.float32),
        grid=(rows // ROW_BLOCK,),
        in_specs=[
            pl.BlockSpec((1, count), lambda i: (0, 0)),
            pl.BlockSpec((count, width), lambda i: (0, 0)),
        ],
        out_specs=pl.BlockSpec((ROW_BLOCK, width), lambda i: (i, 0)),
        name="sum_rows",
    )(index_row, values)


def contract_last(left, right):
    return lax.dot_general(left, right, (((1,), (1,)), ((), ())), preferred_element_type=jnp.float32)


def scorer_kernel(
    column_ref,
    row_ref,
    panel_ref,
    user_ref,
    first_ref,
    bias_one_ref,
    second_ref,
    bias_two_ref,
    last_ref,
    slot_ref,
    user_out_ref,
    user_part,
    user_sum,
    item_grads,
):
    step = pl.program_id(0)
    users, width = user_ref.shape
    slots = panel_ref.shape[0]
    user = user_ref[...]
    user_wide = user.astype(jnp.float32)

    @pl.when(step == 0)
    def _():
        user_part[...] = (
            jnp.dot(user, first_ref[:width, :], preferred_element_type=jnp.float32)
            + bias_one_ref[...]
        )
        user_sum[...] = jnp.zeros_like(user_sum)

    hot = column_ref[0] == lax.broadcasted_iota(jnp.int32, (users, slots), 1)
    item_wide = jnp.dot(
        hot.astype(jnp.float32).astype(jnp.bfloat16),
        panel_ref[...],
        preferred_element_type=jnp.float32,
    )
    item = item_wide.astype(jnp.bfloat16)
    crossed = (user_wide * item_wide).astype(jnp.bfloat16)
    pre_one = (
        jnp.dot(item, first_ref[width : 2 * width, :], preferred_element_type=jnp.float32)
        + jnp.dot(crossed, first_ref[2 * width :, :], preferred_element_type=jnp.float32)
        + user_part[...]
    )
    sig_one = jax.nn.sigmoid(pre_one)
    hid_one = (pre_one * sig_one).astype(jnp.bfloat16)
    second = second_ref[...]
    pre_two = jnp.dot(hid_one, second, preferred_element_type=jnp.float32) + bias_two_ref[...]
    sig_two = jax.nn.sigmoid(pre_two)
    hid_two = (pre_two * sig_two).astype(jnp.bfloat16)
    last = last_ref[...].astype(jnp.float32)
    logits = jnp.sum(hid_two.astype(jnp.float32) * last, axis=1, keepdims=True)
    target = jnp.where(step == 0, 1.0, 0.0)
    logit_grad = loss_scale * (jax.nn.sigmoid(logits) - target)
    delta_two = (logit_grad * last * slope_of(pre_two, sig_two)).astype(jnp.bfloat16)
    delta_one = (contract_last(delta_two, second) * slope_of(pre_one, sig_one)).astype(jnp.bfloat16)
    back_cross = contract_last(delta_one, first_ref[2 * width :, :])
    grads = contract_last(delta_one, first_ref[width : 2 * width, :]) + back_cross * user_wide
    item_grads[pl.ds(pl.multiple_of(step * users, users), users), :] = grads.astype(jnp.bfloat16)
    user_sum[...] += contract_last(delta_one, first_ref[:width, :]) + back_cross * item_wide

    @pl.when(step == pl.num_programs(0) - 1)
    def _():
        user_out_ref[...] = user_sum[...].astype(user_out_ref.dtype)
        index_row = row_ref[...]
        values = item_grads[...]
        for block in range(slots // ROW_BLOCK):
            first = block * ROW_BLOCK
            slot_ref[first : first + ROW_BLOCK, :] = sum_block(index_row, first, values).astype(
                slot_ref.dtype
            )


def run_scorer(pair_slots, panels, users, first_weight, first_bias, second_weight, second_bias, out_weight):
    user_count, per_user = pair_slots.shape
    slots, width = panels.shape
    by_column = pair_slots.T
    hidden_one, hidden_two = second_weight.shape
    whole = lambda *shape: pl.BlockSpec(shape, lambda i: (0,) * len(shape))
    return pl.pallas_call(
        scorer_kernel,
        out_shape=(
            jax.ShapeDtypeStruct((slots, width), jnp.bfloat16),
            jax.ShapeDtypeStruct((user_count, width), jnp.bfloat16),
        ),
        grid=(per_user,),
        in_specs=[
            pl.BlockSpec((1, user_count, 1), lambda i: (i, 0, 0)),
            whole(1, user_count * per_user),
            whole(slots, width),
            whole(user_count, width),
            whole(3 * width, hidden_one),
            whole(1, hidden_one),
            whole(hidden_one, hidden_two),
            whole(1, hidden_two),
            whole(1, hidden_two),
        ],
        out_specs=(whole(slots, width), whole(user_count, width)),
        scratch_shapes=[
            pltpu.VMEM((user_count, hidden_one), jnp.float32),
            pltpu.VMEM((user_count, width), jnp.float32),
            pltpu.VMEM((user_count * per_user, width), jnp.bfloat16),
        ],
        name="run_scorer",
    )(
        by_column.reshape(per_user, user_count, 1),
        by_column.reshape(1, user_count * per_user),
        panels,
        users,
        first_weight,
        first_bias.reshape(1, -1),
        second_weight,
        second_bias.reshape(1, -1),
        out_weight.reshape(1, -1),
    )


def swap(blocks, axis):
    return lax.all_to_all(blocks, axis, split_axis=0, concat_axis=0, tiled=True)


def swap_rows(rows, count):
    width = rows.shape[1]
    return swap(rows.reshape(count, -1, width), BOTH).reshape(-1, width)


def body(
    node_table,
    user_vectors,
    first_weight,
    first_bias,
    second_weight,
    second_bias,
    out_weight,
    panel_rows,
    pair_slots,
):
    count_dp = lax.axis_size("dp")
    count_table = lax.axis_size("table")
    count = count_dp * count_table
    slot_cap = panel_rows.shape[2]
    wanted = panel_rows.reshape(count_dp, count_table, slot_cap).transpose(1, 0, 2)
    wanted = swap(wanted.reshape(count_table, count_dp * slot_cap), "table")
    wanted = wanted.reshape(count_table, count_dp, slot_cap).transpose(1, 0, 2)
    requested = swap(wanted.reshape(count_dp, count_table * slot_cap), "dp").reshape(-1)
    picked = pick_rows(requested, node_table)
    panels = swap_rows(picked, count)
    slot_grads, user_grads = run_scorer(
        pair_slots,
        panels,
        user_vectors,
        first_weight,
        first_bias,
        second_weight,
        second_bias,
        out_weight,
    )
    returned = swap_rows(slot_grads, count)
    grad_table = sum_rows(requested.reshape(1, -1), returned, node_table.shape[0])
    return (grad_table, user_grads)


def solution(mesh):
    placed = (
        P(BOTH, None),
        P(BOTH, None),
        P(),
        P(),
        P(),
        P(),
        P(),
        P(BOTH, None, None),
        P(BOTH, None),
    )
    return jax.shard_map(
        body,
        mesh=mesh,
        in_specs=placed,
        out_specs=(P(BOTH, None), P(BOTH, None)),
        check_vma=False,
    )
```

time: 279 us -> 214 us (0.77)
  blocking collectives: 166 us -> 42.8 us
  waiting for transfers between devices: 25.3 us -> 112 us
  other arithmetic: 36.1 us -> 0.65 us
  Pallas kernels: 0 us -> 27 us
  local copies, waits for them, and re-layouts: 30 us -> 11.4 us
  matrix products: 11.5 us -> 0 us
  starting transfers between devices: 7.31 us -> 18.7 us
    all_to_all x4 -> x2, blocking collectives: 166 us -> 42.8 us  [swap(): return lax.all_to_all(blocks, axis, split_axis=0, concat_axis=0, tiled=True)]
    all_to_all x2, waiting for transfers between devices: 25.3 us -> 112 us  [swap(): return lax.all_to_all(blocks, axis, split_axis=0, concat_axis=0, tiled=True)]
    scatter-add x2 -> x0, other arithmetic: 27.2 us -> none  [the longest x1 13.8 us: body(): jax.ops.segment_sum(item_grads.reshape(-1, feat_width), pair_slots.reshap...]
    pallas_call x0 -> x3, Pallas kernels: none -> 27 us  [the longest x1 17.3 us: run_scorer(): pl.pallas_call(scorer_kernel, out_shape=(jax.ShapeDtypeStruct((slots, wid...]
    gather x2 -> x0, local copies, waits for them, and re-layouts: 15 us -> none  [the longest x1 7.5 us: body(): picked = jnp.take(node_table, safe_rows, axis=0)]
    dot_general x6 -> x0, matrix products: 11.5 us -> none  [the longest x1 6.42 us: run_block(): jnp.dot(delta_first, first_weight.T, preferred_element_type=jnp.float32)]
    all_to_all x2, starting transfers between devices: 7.31 us -> 18.7 us  [swap(): return lax.all_to_all(blocks, axis, split_axis=0, concat_axis=0, tiled=True)]
    all_to_all x5 -> x4, local copies, waits for them, and re-layouts: 5.07 us -> 0.76 us  [swap(): return lax.all_to_all(blocks, axis, split_axis=0, concat_axis=0, tiled=True)]
where the time goes in v1:
time: 214 us; the launch traced here: 213 us
  waiting for transfers between devices  112 us (52%)
  blocking collectives  42.8 us (20%)
  Pallas kernels  27 us (13%)
  starting transfers between devices  18.7 us (9%)
  local copies, waits for them, and re-layouts  11.4 us (5%)
    all_to_all x2, waiting for transfers between devices, swap(): return lax.all_to_all(blocks, axis, split_axis=0, concat_axis=0, tiled=True)  112 us
    all_to_all x2, blocking collectives, swap(): return lax.all_to_all(blocks, axis, split_axis=0, concat_axis=0, tiled=True)  42.8 us
    all_to_all x2, starting transfers between devices, swap(): return lax.all_to_all(blocks, axis, split_axis=0, concat_axis=0, tiled=True)  18.7 us
    pallas_call x1, Pallas kernels, run_scorer(): pl.pallas_call(scorer_kernel, out_shape=(jax.ShapeDtypeStruct((slots, wid...  17.3 us
    reshape x4, local copies, waits for them, and re-layouts, swap_rows(): return swap(rows.reshape(count, -1, width), BOTH).reshape(-1, width)  6.47 us
    pallas_call x1, Pallas kernels, sum_rows(): pl.pallas_call(sum_kernel, out_shape=jax.ShapeDtypeStruct((rows, width),...  4.97 us
    pallas_call x1, Pallas kernels, pick_rows(): pl.pallas_call(pick_kernel, out_shape=jax.ShapeDtypeStruct((count, table....  4.72 us
  transfers between devices with their start and end apart: 2, of which 2 were waited for; matrix products, arithmetic and copies ran while one was open for 2% of the time, Pallas kernels for 0%

profile of v1, /device:TPU:1, one launch (start us, length us, event | category | flops | bytes accessed | tf_op | source)
XLA Modules:
  0.0 213.1 jit_solution(7041635740434700455)
XLA Ops:
  0.6 0.8 reshape.48
  1.5 0.1 copy.17
  1.5 13.8 %all_to_all.28 = s32[16,1,128]{2,1,0:T(1,128)S(1)} all-to-all(s32[16,1,128]{2,1,0:T(1,128)S(1)} %copy.17), channel_id=1, replica_groups=mesh['dp'=32,'table'=16] {'table'}, dimensions={0} | all-to-all | bytes 16384 | tf_op jit(solution)/shard_map/all_to_all | solution.py:193
  15.3 0.1 copy.18
  15.4 0.1 copy.19
  15.5 0.1 copy.20
  15.6 29.0 %all_to_all.29 = s32[32,1,64]{2,1,0:T(1,128)S(1)} all-to-all(s32[32,1,64]{2,1,0:T(1,128)S(1)} %copy.20), channel_id=1, replica_groups=mesh['dp'=32,'table'=16] {'dp'}, dimensions={0} | all-to-all | bytes 16384 | tf_op jit(solution)/shard_map/all_to_all | solution.py:193
  44.6 0.7 reshape_reshape.7.index_ref
  45.2 4.7 %pick_rows.1 = bf16[2048,256]{1,0:T(8,128)(2,1)} custom-call(s32[16,128]{1,0:T(8,128)} %reshape_reshape.7.index_ref, bf16[2048,256]{1,0:T(8,128)(2,1)} %table_ref.1), custom_call_target="tpu_custom_call" | custom-call | tf_op jit(solution)/shard_map/pick_rows/pallas_call | solution.py:36
  50.0 0.0 copy-start
  50.0 2.1 %reshape.52 = bf16[512,4,256]{2,1,0:T(4,128)(2,1)} reshape(bf16[2048,256]{1,0:T(8,128)(2,1)} %pick_rows.1) | data formatting | bytes 2097152 | tf_op jit(solution)/shard_map/reshape | solution.py:198
  52.1 9.1 %all-to-all-start.2 = ((bf16[512,4,256]{2,1,0:T(4,128)(2,1)}), bf16[512,4,256]{2,1,0:T(4,128)(2,1)S(1)}, u32[]{:S(2)}, u32[]{:S(2)}) async-start(bf16[512,4,256]{2,1,0:T(4,128)(2,1)} %reshape.52), calls=%async_computation.2 | async-start | bytes 2097152 | tf_op jit(solution)/shard_map/all_to_all | solution.py:193
  61.2 0.0 copy-done
  61.3 0.6 copy.22
  61.9 1.3 copy.21.column_ref
  63.2 55.9 %all-to-all-done.2 = bf16[512,4,256]{2,1,0:T(4,128)(2,1)S(1)} async-done(((bf16[512,4,256]{2,1,0:T(4,128)(2,1)}), bf16[512,4,256]{2,1,0:T(4,128)(2,1)S(1)}, u32[]{:S(2)}, u32[]{:S(2)}) %all-to-all-start.2) | async-done | bytes 1048608 | tf_op jit(solution)/shard_map/all_to_all | solution.py:193
  119.1 1.1 reshape.53.panel_ref
  120.2 17.3 %run_scorer.1 = (bf16[2048,256]{1,0:T(8,128)(2,1)}, bf16[256,256]{1,0:T(8,128)(2,1)}) custom-call(s32[8,256,1]{2,1,0:T(8,128)} %copy.21.column_ref, s32[1,2048]{1,0:T(1,128)} %bitcast.25, bf16[2048,256]{1,0:T(8,128)(2,1)} %reshape.53.panel_ref, bf16[256,256]{1,0:T(8,128)(2,1)} %user_ref.1, bf16[768,256]{1,0:T(8,128)(2,1)} %first_ref.1, f32[1,256]{1,0:T(1,128)} %bitcast.26, ...), custom_call_target="tpu_custom_call" | custom-call | tf_op jit(solution)/shard_map/run_scorer/pallas_call | solution.py:154
  137.5 2.1 %reshape.57 = bf16[512,4,256]{2,1,0:T(4,128)(2,1)} reshape(bf16[2048,256]{1,0:T(8,128)(2,1)} %get-tuple-element.4) | data formatting | bytes 2097152 | tf_op jit(solution)/shard_map/reshape | solution.py:198
  139.6 9.6 %all-to-all-start.3 = ((bf16[512,4,256]{2,1,0:T(4,128)(2,1)}), bf16[512,4,256]{2,1,0:T(4,128)(2,1)S(1)}, u32[]{:S(2)}, u32[]{:S(2)}) async-start(bf16[512,4,256]{2,1,0:T(4,128)(2,1)} %reshape.57), calls=%async_computation.3 | async-start | bytes 2097152 | tf_op jit(solution)/shard_map/all_to_all | solution.py:193
  149.2 0.5 broadcast.5
  149.7 0.6 reduce.5
  150.4 0.7 reshape_reshape.6.index_ref
  151.1 55.9 %all-to-all-done.3 = bf16[512,4,256]{2,1,0:T(4,128)(2,1)S(1)} async-done(((bf16[512,4,256]{2,1,0:T(4,128)(2,1)}), bf16[512,4,256]{2,1,0:T(4,128)(2,1)S(1)}, u32[]{:S(2)}, u32[]{:S(2)}) %all-to-all-start.3) | async-done | bytes 1048608 | tf_op jit(solution)/shard_map/all_to_all | solution.py:193
  207.0 1.1 reshape.58.value_ref
  208.1 5.0 %sum_rows.1 = f32[2048,256]{1,0:T(8,128)} custom-call(s32[1,2048]{1,0:T(1,128)} %reshape_reshape.6.index_ref, bf16[2048,256]{1,0:T(8,128)(2,1)} %reshape.58.value_ref), custom_call_target="tpu_custom_call" | custom-call | tf_op jit(solution)/shard_map/sum_rows/pallas_call | solution.py:59
  (1 shorter events, 0.0 us)
Async XLA Ops:
  50.0 11.3 %copy-start = (s32[256,8]{0,1:T(8,128)S(1)}, s32[256,8]{0,1:T(8,128)}, u32[]{:S(2)}) copy-start(s32[256,8]{0,1:T(8,128)} %param.17) | copy-start | bytes 24580
  52.1 66.9 %all-to-all-start.2 = ((bf16[512,4,256]{2,1,0:T(4,128)(2,1)}), bf16[512,4,256]{2,1,0:T(4,128)(2,1)S(1)}, u32[]{:S(2)}, u32[]{:S(2)}) async-start(bf16[512,4,256]{2,1,0:T(4,128)(2,1)} %reshape.52), calls=%async_computation.2 | async-start | bytes 2097152 | tf_op jit(solution)/shard_map/all_to_all | solution.py:193
  139.6 67.4 %all-to-all-start.3 = ((bf16[512,4,256]{2,1,0:T(4,128)(2,1)}), bf16[512,4,256]{2,1,0:T(4,128)(2,1)S(1)}, u32[]{:S(2)}, u32[]{:S(2)}) async-start(bf16[512,4,256]{2,1,0:T(4,128)(2,1)} %reshape.57), calls=%async_computation.3 | async-start | bytes 2097152 | tf_op jit(solution)/shard_map/all_to_all | solution.py:193

commit v2 on v1

v2 whole, which is shorter than its diff:
```python
import jax
import jax.numpy as jnp
from jax import lax
from jax.experimental import pallas as pl
from jax.experimental.pallas import tpu as pltpu
from jax.sharding import PartitionSpec as P

loss_scale = 32.0
BOTH = ("dp", "table")
ROW_BLOCK = 512
PAIR_BLOCK = 512
PICK_BLOCK = 512


def slope_of(value, sig):
    return sig * (1.0 + value * (1.0 - sig))


def contract_last(left, right):
    return lax.dot_general(left, right, (((1,), (1,)), ((), ())), preferred_element_type=jnp.float32)


def low_half(rows):
    return lax.broadcasted_iota(jnp.int32, (rows, 8, 128), 1) < 4


def to_tiles(rows):
    groups = rows.shape[0] // 8
    parts = rows.reshape(groups, 8, 256)
    left, right = parts[:, :, :128], parts[:, :, 128:]
    low = low_half(groups)
    even = jnp.where(low, left, pltpu.roll(right, 4, 1))
    odd = jnp.where(low, pltpu.roll(left, 4, 1), right)
    return even, odd


def from_tiles(even, odd):
    groups = even.shape[0]
    low = low_half(groups)
    left = jnp.where(low, even, pltpu.roll(odd, 4, 1))
    right = jnp.where(low, pltpu.roll(even, 4, 1), odd)
    return left.reshape(groups * 8, 128), right.reshape(groups * 8, 128)


def unpack_tiles(tile_ref, out_ref):
    block = 64
    for first in range(0, tile_ref.shape[0], block):
        even = tile_ref[first : first + block, 0].astype(jnp.float32)
        odd = tile_ref[first : first + block, 1].astype(jnp.float32)
        left, right = from_tiles(even, odd)
        out_ref[8 * first : 8 * (first + block), :128] = left.astype(out_ref.dtype)
        out_ref[8 * first : 8 * (first + block), 128:] = right.astype(out_ref.dtype)


def store_tiles(rows, first, out_ref):
    even, odd = to_tiles(rows)
    at = first // 8
    out_ref[at : at + even.shape[0], 0] = even.astype(out_ref.dtype)
    out_ref[at : at + even.shape[0], 1] = odd.astype(out_ref.dtype)


def pick_block(columns, first, count, table):
    part = columns.shape[0]
    hot = []
    for at in range(first // part, (first + count) // part):
        ids = lax.broadcasted_iota(jnp.int32, (part, table.shape[0]), 1)
        hot.append((columns[:, at : at + 1] == ids).astype(jnp.float32).astype(jnp.bfloat16))
    return jnp.dot(jnp.concatenate(hot, axis=0), table, preferred_element_type=jnp.float32)


def sum_block(index_row, first, values):
    count = index_row.shape[1]
    row_id = lax.broadcasted_iota(jnp.int32, (ROW_BLOCK, count), 0) + first
    hot = (row_id == index_row).astype(jnp.float32).astype(jnp.bfloat16)
    return jnp.dot(hot, values, preferred_element_type=jnp.float32)


VMEM = pl.BlockSpec(memory_space=pltpu.VMEM)


def pick_kernel(index_ref, table_ref, out_ref):
    table = table_ref[...]
    columns = index_ref[...].T
    for first in range(0, index_ref.size, PICK_BLOCK):
        store_tiles(pick_block(columns, first, PICK_BLOCK, table), first, out_ref)


def pick_rows(index, table):
    return pl.pallas_call(
        pick_kernel,
        out_shape=jax.ShapeDtypeStruct((index.size // 8, 2, 8, 128), table.dtype),
        in_specs=[VMEM] * 2,
        out_specs=VMEM,
        name="pick_rows",
        compiler_params=pltpu.CompilerParams(vmem_limit_bytes=24 << 20),
    )(index.reshape(-1, 64), table)


def sum_kernel(index_ref, tile_ref, out_ref, values):
    @pl.when(pl.program_id(0) == 0)
    def _():
        unpack_tiles(tile_ref, values)

    first = pl.program_id(0) * ROW_BLOCK
    out_ref[...] = sum_block(index_ref[...], first, values[...])


def sum_rows(index_row, tiles, rows):
    count = index_row.shape[1]
    return pl.pallas_call(
        sum_kernel,
        out_shape=jax.ShapeDtypeStruct((rows, 256), jnp.float32),
        grid=(rows // ROW_BLOCK,),
        in_specs=[
            pl.BlockSpec((1, count), lambda i: (0, 0)),
            pl.BlockSpec(tiles.shape, lambda i: (0, 0, 0, 0)),
        ],
        out_specs=pl.BlockSpec((ROW_BLOCK, 256), lambda i: (i, 0)),
        scratch_shapes=[pltpu.VMEM((count, 256), tiles.dtype)],
        name="sum_rows",
        compiler_params=pltpu.CompilerParams(vmem_limit_bytes=24 << 20),
    )(index_row, tiles)


def scorer_kernel(
    index_ref,
    row_ref,
    tile_ref,
    user_ref,
    first_ref,
    bias_one_ref,
    second_ref,
    bias_two_ref,
    last_ref,
    slot_ref,
    user_out_ref,
    panel_ref,
    item_grads,
):
    users, width = user_ref.shape
    pairs = index_ref.size
    slots = panel_ref.shape[0]
    unpack_tiles(tile_ref, panel_ref)
    panels = panel_ref[...]
    columns = index_ref[...].T
    user = user_ref[...]
    last = last_ref[...].astype(jnp.float32)
    second = second_ref[...]
    weight_user = first_ref[:width, :]
    weight_item = first_ref[width : 2 * width, :]
    weight_cross = first_ref[2 * width :, :]
    repeat = PAIR_BLOCK // users
    user_wide = jnp.concatenate([user.astype(jnp.float32)] * repeat, axis=0)
    user_part = jnp.dot(user, weight_user, preferred_element_type=jnp.float32) + bias_one_ref[...]
    user_part = jnp.concatenate([user_part] * repeat, axis=0)

    def fold(block):
        total = block[:users]
        for at in range(1, repeat):
            total = total + block[at * users : (at + 1) * users]
        return total

    delta_sum = jnp.zeros((users, width), jnp.float32)
    cross_sum = jnp.zeros((users, width), jnp.float32)
    ahead = pick_block(columns, 0, PAIR_BLOCK, panels)
    for first in range(0, pairs, PAIR_BLOCK):
        item_wide = ahead
        if first + PAIR_BLOCK < pairs:
            ahead = pick_block(columns, first + PAIR_BLOCK, PAIR_BLOCK, panels)
        item = item_wide.astype(jnp.bfloat16)
        crossed = (user_wide * item_wide).astype(jnp.bfloat16)
        pre_one = (
            jnp.dot(item, weight_item, preferred_element_type=jnp.float32)
            + jnp.dot(crossed, weight_cross, preferred_element_type=jnp.float32)
            + user_part
        )
        sig_one = jax.nn.sigmoid(pre_one)
        hid_one = (pre_one * sig_one).astype(jnp.bfloat16)
        pre_two = jnp.dot(hid_one, second, preferred_element_type=jnp.float32) + bias_two_ref[...]
        sig_two = jax.nn.sigmoid(pre_two)
        hid_two = (pre_two * sig_two).astype(jnp.bfloat16)
        logits = jnp.sum(hid_two.astype(jnp.float32) * last, axis=1, keepdims=True)
        logit_grad = jax.nn.sigmoid(logits)
        if first == 0:
            place = lax.broadcasted_iota(jnp.int32, logits.shape, 0)
            logit_grad = logit_grad - jnp.where(place < users, 1.0, 0.0)
        logit_grad = loss_scale * logit_grad
        delta_two = (logit_grad * last * slope_of(pre_two, sig_two)).astype(jnp.bfloat16)
        delta_one = contract_last(delta_two, second) * slope_of(pre_one, sig_one)
        delta_one = delta_one.astype(jnp.bfloat16)
        back_cross = contract_last(delta_one, weight_cross)
        grads = contract_last(delta_one, weight_item) + back_cross * user_wide
        item_grads[first : first + PAIR_BLOCK, :] = grads.astype(jnp.bfloat16)
        delta_sum = delta_sum + fold(delta_one.astype(jnp.float32))
        cross_sum = cross_sum + fold(back_cross * item_wide)
    delta_high = delta_sum.astype(jnp.bfloat16)
    delta_low = (delta_sum - delta_high.astype(jnp.float32)).astype(jnp.bfloat16)
    user_grads = contract_last(delta_high, weight_user) + contract_last(delta_low, weight_user)
    user_out_ref[...] = (user_grads + cross_sum).astype(user_out_ref.dtype)
    index_row = row_ref[...]
    values = item_grads[...]
    for first in range(0, slots, ROW_BLOCK):
        store_tiles(sum_block(index_row, first, values), first, slot_ref)


def run_scorer(pair_slots, tiles, users, first_weight, first_bias, second_weight, second_bias, out_weight):
    pairs = pair_slots.size
    width = users.shape[1]
    by_column = pair_slots.T
    return pl.pallas_call(
        scorer_kernel,
        out_shape=(
            jax.ShapeDtypeStruct(tiles.shape, jnp.bfloat16),
            jax.ShapeDtypeStruct(users.shape, jnp.bfloat16),
        ),
        in_specs=[VMEM] * 9,
        out_specs=(VMEM, VMEM),
        scratch_shapes=[
            pltpu.VMEM((tiles.size // width, width), jnp.bfloat16),
            pltpu.VMEM((pairs, width), jnp.bfloat16),
        ],
        name="run_scorer",
        compiler_params=pltpu.CompilerParams(vmem_limit_bytes=24 << 20),
    )(
        by_column.reshape(pairs // 128, 128),
        by_column.reshape(1, pairs),
        tiles,
        users,
        first_weight,
        first_bias.reshape(1, -1),
        second_weight,
        second_bias.reshape(1, -1),
        out_weight.reshape(1, -1),
    )


def swap(blocks, axis):
    return lax.all_to_all(blocks, axis, split_axis=0, concat_axis=0, tiled=True)


def swap_tiles(tiles, count):
    return swap(tiles.reshape(count, -1, 128), BOTH).reshape(tiles.shape)


def body(
    node_table,
    user_vectors,
    first_weight,
    first_bias,
    second_weight,
    second_bias,
    out_weight,
    panel_rows,
    pair_slots,
):
    count_dp = lax.axis_size("dp")
    count_table = lax.axis_size("table")
    count = count_dp * count_table
    slot_cap = panel_rows.shape[2]
    wanted = panel_rows.reshape(count_dp, count_table, slot_cap).transpose(1, 0, 2)
    wanted = swap(wanted.reshape(count_table, count_dp * slot_cap), "table")
    wanted = wanted.reshape(count_table, count_dp, slot_cap).transpose(1, 0, 2)
    requested = swap(wanted.reshape(count_dp, count_table * slot_cap), "dp")
    panels = swap_tiles(pick_rows(requested, node_table), count)
    slot_grads, user_grads = run_scorer(
        pair_slots,
        panels,
        user_vectors,
        first_weight,
        first_bias,
        second_weight,
        second_bias,
        out_weight,
    )
    returned = swap_tiles(slot_grads, count)
    grad_table = sum_rows(requested.reshape(1, -1), returned, node_table.shape[0])
    return (grad_table, user_grads)


def solution(mesh):
    placed = (
        P(BOTH, None),
        P(BOTH, None),
        P(),
        P(),
        P(),
        P(),
        P(),
        P(BOTH, None, None),
        P(BOTH, None),
    )
    return jax.shard_map(
        body,
        mesh=mesh,
        in_specs=placed,
        out_specs=(P(BOTH, None), P(BOTH, None)),
        check_vma=False,
    )
```

time: 214 us -> 197 us (0.921)
  Pallas kernels: 27 us -> 16 us
  local copies, waits for them, and re-layouts: 11.4 us -> 3.02 us
    pallas_call x3, Pallas kernels: 27 us -> 16 us  [the longest x1 8.45 us: run_scorer(): pl.pallas_call(scorer_kernel, out_shape=(jax.ShapeDtypeStruct(tiles.shape...]
    reshape x5 -> x2, local copies, waits for them, and re-layouts: 7.81 us -> 0.08 us  [the longest x1 0.08 us: body(): requested.reshape(1, -1)]
    all_to_all x2, waiting for transfers between devices: 112 us -> 114 us  [swap(): return lax.all_to_all(blocks, axis, split_axis=0, concat_axis=0, tiled=True)]
  transfers between devices with their start and end apart: 2 -> 2, of which waited for: 2 -> 2; matrix products, arithmetic and copies ran while one was open for 2% -> 1% of each run, Pallas kernels for 0% -> 0%
where the time goes in v2:
time: 197 us; the launch traced here: 196 us
  waiting for transfers between devices  114 us (58%)
  blocking collectives  42.8 us (22%)
  starting transfers between devices  18.7 us (9%)
  Pallas kernels  16 us (8%)
  local copies, waits for them, and re-layouts  3.02 us (2%)
    all_to_all x2, waiting for transfers between devices, swap(): return lax.all_to_all(blocks, axis, split_axis=0, concat_axis=0, tiled=True)  114 us
    all_to_all x2, blocking collectives, swap(): return lax.all_to_all(blocks, axis, split_axis=0, concat_axis=0, tiled=True)  42.8 us
    all_to_all x2, starting transfers between devices, swap(): return lax.all_to_all(blocks, axis, split_axis=0, concat_axis=0, tiled=True)  18.7 us
    pallas_call x1, Pallas kernels, run_scorer(): pl.pallas_call(scorer_kernel, out_shape=(jax.ShapeDtypeStruct(tiles.shape...  8.45 us
    pallas_call x1, Pallas kernels, sum_rows(): pl.pallas_call(sum_kernel, out_shape=jax.ShapeDtypeStruct((rows, 256), jn...  4.07 us
  transfers between devices with their start and end apart: 2, of which 2 were waited for; matrix products, arithmetic and copies ran while one was open for 1% of the time, Pallas kernels for 0%

profile of v2, /device:TPU:1, one launch (start us, length us, event | category | flops | bytes accessed | tf_op | source)
XLA Modules:
  0.0 196.3 jit_solution(11195737355319525070)
XLA Ops:
  0.6 0.8 reshape.50
  1.5 0.1 copy.15
  1.5 13.8 %all_to_all.30 = s32[16,1,128]{2,1,0:T(1,128)S(1)} all-to-all(s32[16,1,128]{2,1,0:T(1,128)S(1)} %copy.15), channel_id=1, replica_groups=mesh['dp'=32,'table'=16] {'table'}, dimensions={0} | all-to-all | bytes 16384 | tf_op jit(solution)/shard_map/all_to_all | solution.py:238
  15.3 0.1 copy.16
  15.4 0.1 copy.17
  15.5 0.1 copy.18
  15.6 29.0 %all_to_all.31 = s32[32,1,64]{2,1,0:T(1,128)S(1)} all-to-all(s32[32,1,64]{2,1,0:T(1,128)S(1)} %copy.18), channel_id=1, replica_groups=mesh['dp'=32,'table'=16] {'dp'}, dimensions={0} | all-to-all | bytes 16384 | tf_op jit(solution)/shard_map/all_to_all | solution.py:238
  44.6 0.0 copy-start
  44.6 1.2 copy-done
  45.8 0.0 copy-start.7
  45.8 0.0 copy-start.1
  45.8 0.0 copy-start.2
  45.8 0.0 copy-start.3
  45.8 0.0 copy-start.4
  45.8 0.0 copy-start.5
  45.8 0.0 copy-start.6
  45.8 3.5 %pick_rows.1 = bf16[256,2,8,128]{3,2,1,0:T(8,128)(2,1)} custom-call(s32[32,64]{1,0:T(8,128)S(1)} %bitcast.22, bf16[2048,256]{1,0:T(8,128)(2,1)S(1)} %copy-done), custom_call_target="tpu_custom_call" | custom-call | tf_op jit(solution)/shard_map/pick_rows/pallas_call | solution.py:89
  49.4 9.2 %all-to-all-start.2 = ((bf16[512,8,128]{2,1,0:T(8,128)(2,1)}), bf16[512,8,128]{2,1,0:T(8,128)(2,1)S(1)}, u32[]{:S(2)}, u32[]{:S(2)}) async-start(bf16[512,8,128]{2,1,0:T(8,128)(2,1)} %bitcast.7), calls=%async_computation.2 | async-start | bytes 2097152 | tf_op jit(solution)/shard_map/all_to_all | solution.py:238
  58.5 0.0 copy-done.7
  58.6 57.8 %all-to-all-done.2 = bf16[512,8,128]{2,1,0:T(8,128)(2,1)S(1)} async-done(((bf16[512,8,128]{2,1,0:T(8,128)(2,1)}), bf16[512,8,128]{2,1,0:T(8,128)(2,1)S(1)}, u32[]{:S(2)}, u32[]{:S(2)}) %all-to-all-start.2) | async-done | bytes 1048608 | tf_op jit(solution)/shard_map/all_to_all | solution.py:238
  116.3 0.0 copy-done.1
  116.3 0.0 copy-done.2
  116.3 0.0 copy-done.3
  116.3 0.0 copy-done.4
  116.3 0.0 copy-done.5
  116.4 0.0 copy-done.6
  116.4 8.4 %run_scorer.1 = (bf16[256,2,8,128]{3,2,1,0:T(8,128)(2,1)}, bf16[256,256]{1,0:T(8,128)(2,1)}) custom-call(s32[16,128]{1,0:T(8,128)S(1)} %reshape.53.index_ref, s32[1,2048]{1,0:T(1,128)S(1)} %bitcast.23, bf16[256,2,8,128]{3,2,1,0:T(8,128)(2,1)S(1)} %bitcast.21, bf16[256,256]{1,0:T(8,128)(2,1)S(1)} %copy-done.2, bf16[768,256]{1,0:T(8,128)(2,1)S(1)} %copy-done.1, ...), custom_call_target="tpu_custom_call" | custom-call | tf_op jit(solution)/shard_map/run_scorer/pallas_call | solution.py:210
  124.8 9.6 %all-to-all-start.3 = ((bf16[512,8,128]{2,1,0:T(8,128)(2,1)}), bf16[512,8,128]{2,1,0:T(8,128)(2,1)S(1)}, u32[]{:S(2)}, u32[]{:S(2)}) async-start(bf16[512,8,128]{2,1,0:T(8,128)(2,1)} %bitcast.12), calls=%async_computation.3 | async-start | bytes 2097152 | tf_op jit(solution)/shard_map/all_to_all | solution.py:238
  134.4 0.5 broadcast.3
  134.9 0.7 reduce.3
  135.6 0.1 reshape.52.index_ref
  135.7 56.5 %all-to-all-done.3 = bf16[512,8,128]{2,1,0:T(8,128)(2,1)S(1)} async-done(((bf16[512,8,128]{2,1,0:T(8,128)(2,1)}), bf16[512,8,128]{2,1,0:T(8,128)(2,1)S(1)}, u32[]{:S(2)}, u32[]{:S(2)}) %all-to-all-start.3) | async-done | bytes 1048608 | tf_op jit(solution)/shard_map/all_to_all | solution.py:238
  192.2 4.1 %sum_rows.1 = f32[2048,256]{1,0:T(8,128)} custom-call(s32[1,2048]{1,0:T(1,128)S(1)} %reshape.52.index_ref, bf16[256,2,8,128]{3,2,1,0:T(8,128)(2,1)S(1)} %bitcast.20), custom_call_target="tpu_custom_call" | custom-call | tf_op jit(solution)/shard_map/sum_rows/pallas_call | solution.py:110
  (3 shorter events, 0.1 us)
Async XLA Ops:
  44.6 1.2 copy-start
  45.8 12.7 %copy-start.7 = (s32[256,8]{0,1:T(8,128)S(1)}, s32[256,8]{0,1:T(8,128)}, u32[]{:S(2)}) copy-start(s32[256,8]{0,1:T(8,128)} %param.17) | copy-start | bytes 24580
  45.8 70.5 %copy-start.1 = (bf16[768,256]{1,0:T(8,128)(2,1)S(1)}, bf16[768,256]{1,0:T(8,128)(2,1)}, u32[]{:S(2)}) copy-start(bf16[768,256]{1,0:T(8,128)(2,1)} %first_ref.1) | copy-start | bytes 1179652
  45.8 70.5 %copy-start.2 = (bf16[256,256]{1,0:T(8,128)(2,1)S(1)}, bf16[256,256]{1,0:T(8,128)(2,1)}, u32[]{:S(2)}) copy-start(bf16[256,256]{1,0:T(8,128)(2,1)} %user_ref.1) | copy-start | bytes 393220
  45.8 70.5 %copy-start.3 = (bf16[256,128]{1,0:T(8,128)(2,1)S(1)}, bf16[256,128]{1,0:T(8,128)(2,1)}, u32[]{:S(2)}) copy-start(bf16[256,128]{1,0:T(8,128)(2,1)} %second_ref.1) | copy-start | bytes 196612
  45.8 70.5 %copy-start.4 = (f32[256]{0:T(256)S(1)}, f32[256]{0:T(256)}, u32[]{:S(2)}) copy-start(f32[256]{0:T(256)} %param.12) | copy-start | bytes 3076
  45.8 70.5 %copy-start.5 = (f32[128]{0:T(128)S(1)}, f32[128]{0:T(128)}, u32[]{:S(2)}) copy-start(f32[128]{0:T(128)} %param.14) | copy-start | bytes 1540
  45.8 70.5 %copy-start.6 = (bf16[128]{0:T(256)(128)(2,1)S(1)}, bf16[128]{0:T(256)(128)(2,1)}, u32[]{:S(2)}) copy-start(bf16[128]{0:T(256)(128)(2,1)} %param.15) | copy-start | bytes 772
  49.4 67.0 %all-to-all-start.2 = ((bf16[512,8,128]{2,1,0:T(8,128)(2,1)}), bf16[512,8,128]{2,1,0:T(8,128)(2,1)S(1)}, u32[]{:S(2)}, u32[]{:S(2)}) async-start(bf16[512,8,128]{2,1,0:T(8,128)(2,1)} %bitcast.7), calls=%async_computation.2 | async-start | bytes 2097152 | tf_op jit(solution)/shard_map/all_to_all | solution.py:238
  124.8 67.4 %all-to-all-start.3 = ((bf16[512,8,128]{2,1,0:T(8,128)(2,1)}), bf16[512,8,128]{2,1,0:T(8,128)(2,1)S(1)}, u32[]{:S(2)}, u32[]{:S(2)}) async-start(bf16[512,8,128]{2,1,0:T(8,128)(2,1)} %bitcast.12), calls=%async_computation.3 | async-start | bytes 2097152 | tf_op jit(solution)/shard_map/all_to_all | solution.py:238

commit v3 on v2

--- a/solution.py
+++ b/solution.py
@@ -83,6 +83,22 @@
     columns = index_ref[...].T
     for first in range(0, index_ref.size, PICK_BLOCK):
         store_tiles(pick_block(columns, first, PICK_BLOCK, table), first, out_ref)
+
+
+def stage_kernel(table_ref, out_ref):
+    out_ref[...] = table_ref[...]
+
+
+def stage_table(table):
+    return pl.pallas_call(
+        stage_kernel,
+        out_shape=jax.ShapeDtypeStruct(table.shape, table.dtype),
+        in_specs=[VMEM],
+        out_specs=VMEM,
+        name="stage_table",
+        compiler_params=pltpu.CompilerParams(vmem_limit_bytes=8 << 20),
+        cost_estimate=pl.CostEstimate(flops=0, bytes_accessed=2 * table.size * 2, transcendentals=0),
+    )(table)
 
 
 def pick_rows(index, table):
@@ -261,7 +277,7 @@
     wanted = swap(wanted.reshape(count_table, count_dp * slot_cap), "table")
     wanted = wanted.reshape(count_table, count_dp, slot_cap).transpose(1, 0, 2)
     requested = swap(wanted.reshape(count_dp, count_table * slot_cap), "dp")
-    panels = swap_tiles(pick_rows(requested, node_table), count)
+    panels = swap_tiles(pick_rows(requested, stage_table(node_table)), count)
     slot_grads, user_grads = run_scorer(
         pair_slots,
         panels,

time: 197 us -> 196 us (level)
  blocking collectives: 42.8 us -> 13.8 us
  starting transfers between devices: 18.7 us -> 36.1 us
  waiting for transfers between devices: 114 us -> 125 us
    all_to_all x2 -> x1, blocking collectives: 42.8 us -> 13.8 us  [swap(): return lax.all_to_all(blocks, axis, split_axis=0, concat_axis=0, tiled=True)]
    all_to_all x2 -> x3, starting transfers between devices: 18.7 us -> 36.1 us  [swap(): return lax.all_to_all(blocks, axis, split_axis=0, concat_axis=0, tiled=True)]
    all_to_all x2 -> x3, waiting for transfers between devices: 114 us -> 125 us  [swap(): return lax.all_to_all(blocks, axis, split_axis=0, concat_axis=0, tiled=True)]
  transfers between devices with their start and end apart: 2 -> 3, of which waited for: 2 -> 3; matrix products, arithmetic and copies ran while one was open for 1% -> 1% of each run, Pallas kernels for 0% -> 0%
where the time goes in v3:
time: 196 us
  waiting for transfers between devices  125 us (64%)
  starting transfers between devices  36.1 us (18%)
  Pallas kernels  16.1 us (8%)
  blocking collectives  13.8 us (7%)
  local copies, waits for them, and re-layouts  3.63 us (2%)
    all_to_all x3, waiting for transfers between devices, swap(): return lax.all_to_all(blocks, axis, split_axis=0, concat_axis=0, tiled=True)  125 us
    all_to_all x3, starting transfers between devices, swap(): return lax.all_to_all(blocks, axis, split_axis=0, concat_axis=0, tiled=True)  36.1 us
    all_to_all x1, blocking collectives, swap(): return lax.all_to_all(blocks, axis, split_axis=0, concat_axis=0, tiled=True)  13.8 us
    pallas_call x1, Pallas kernels, run_scorer(): pl.pallas_call(scorer_kernel, out_shape=(jax.ShapeDtypeStruct(tiles.shape...  8.43 us
    pallas_call x1, Pallas kernels, sum_rows(): pl.pallas_call(sum_kernel, out_shape=jax.ShapeDtypeStruct((rows, 256), jn...  4.07 us
  transfers between devices with their start and end apart: 3, of which 3 were waited for; matrix products, arithmetic and copies ran while one was open for 1% of the time, Pallas kernels for 0%

profile of v3, /device:TPU:1, one launch (start us, length us, event | category | flops | bytes accessed | tf_op | source)
XLA Modules:
  0.0 195.8 jit_solution(806716562984544640)
XLA Ops:
  0.6 0.8 reshape.50
  1.5 0.1 copy.15
  1.5 13.8 %all_to_all.30 = s32[16,1,128]{2,1,0:T(1,128)S(1)} all-to-all(s32[16,1,128]{2,1,0:T(1,128)S(1)} %copy.15), channel_id=1, replica_groups=mesh['dp'=32,'table'=16] {'table'}, dimensions={0} | all-to-all | bytes 16384 | tf_op jit(solution)/shard_map/all_to_all | solution.py:254
  15.3 0.1 copy.16
  15.4 0.1 copy.17
  15.5 0.7 copy.18
  16.2 17.3 %all-to-all-start.1 = ((s32[32,1,64]{2,1,0:T(1,128)}), s32[32,1,64]{2,1,0:T(1,128)S(1)}, u32[]{:S(2)}, u32[]{:S(2)}) async-start(s32[32,1,64]{2,1,0:T(1,128)} %copy.18), calls=%async_computation.1 | async-start | bytes 32768 | tf_op jit(solution)/shard_map/all_to_all | solution.py:254
  33.6 0.0 copy-start
  33.6 1.2 copy-done
  34.8 0.1 stage_table.1.table_ref
  34.9 10.4 %all-to-all-done.1 = s32[32,1,64]{2,1,0:T(1,128)S(1)} async-done(((s32[32,1,64]{2,1,0:T(1,128)}), s32[32,1,64]{2,1,0:T(1,128)S(1)}, u32[]{:S(2)}, u32[]{:S(2)}) %all-to-all-start.1) | async-done | bytes 8224 | tf_op jit(solution)/shard_map/all_to_all | solution.py:254
  45.3 0.0 copy-start.7
  45.3 0.0 copy-start.1
  45.3 0.0 copy-start.2
  45.3 0.0 copy-start.3
  45.3 0.0 copy-start.4
  45.3 0.0 copy-start.5
  45.4 0.0 copy-start.6
  45.4 3.5 %pick_rows.1 = bf16[256,2,8,128]{3,2,1,0:T(8,128)(2,1)} custom-call(s32[32,64]{1,0:T(8,128)S(1)} %bitcast.22, bf16[2048,256]{1,0:T(8,128)(2,1)S(1)} %stage_table.1.table_ref), custom_call_target="tpu_custom_call" | custom-call | tf_op jit(solution)/shard_map/pick_rows/pallas_call | solution.py:105
  48.9 9.2 %all-to-all-start.2 = ((bf16[512,8,128]{2,1,0:T(8,128)(2,1)}), bf16[512,8,128]{2,1,0:T(8,128)(2,1)S(1)}, u32[]{:S(2)}, u32[]{:S(2)}) async-start(bf16[512,8,128]{2,1,0:T(8,128)(2,1)} %bitcast.7), calls=%async_computation.2 | async-start | bytes 2097152 | tf_op jit(solution)/shard_map/all_to_all | solution.py:254
  58.0 0.0 copy-done.7
  58.1 57.8 %all-to-all-done.2 = bf16[512,8,128]{2,1,0:T(8,128)(2,1)S(1)} async-done(((bf16[512,8,128]{2,1,0:T(8,128)(2,1)}), bf16[512,8,128]{2,1,0:T(8,128)(2,1)S(1)}, u32[]{:S(2)}, u32[]{:S(2)}) %all-to-all-start.2) | async-done | bytes 1048608 | tf_op jit(solution)/shard_map/all_to_all | solution.py:254
  115.8 0.0 copy-done.1
  115.8 0.0 copy-done.2
  115.8 0.0 copy-done.3
  115.9 0.0 copy-done.4
  115.9 0.0 copy-done.5
  115.9 0.0 copy-done.6
  115.9 8.4 %run_scorer.1 = (bf16[256,2,8,128]{3,2,1,0:T(8,128)(2,1)}, bf16[256,256]{1,0:T(8,128)(2,1)}) custom-call(s32[16,128]{1,0:T(8,128)S(1)} %reshape.53.index_ref, s32[1,2048]{1,0:T(1,128)S(1)} %bitcast.23, bf16[256,2,8,128]{3,2,1,0:T(8,128)(2,1)S(1)} %bitcast.21, bf16[256,256]{1,0:T(8,128)(2,1)S(1)} %copy-done.2, bf16[768,256]{1,0:T(8,128)(2,1)S(1)} %copy-done.1, ...), custom_call_target="tpu_custom_call" | custom-call | tf_op jit(solution)/shard_map/run_scorer/pallas_call | solution.py:226
  124.3 9.6 %all-to-all-start.3 = ((bf16[512,8,128]{2,1,0:T(8,128)(2,1)}), bf16[512,8,128]{2,1,0:T(8,128)(2,1)S(1)}, u32[]{:S(2)}, u32[]{:S(2)}) async-start(bf16[512,8,128]{2,1,0:T(8,128)(2,1)} %bitcast.12), calls=%async_computation.3 | async-start | bytes 2097152 | tf_op jit(solution)/shard_map/all_to_all | solution.py:254
  133.9 0.5 broadcast.3
  134.4 0.7 reduce.3
  135.1 0.1 reshape.52.index_ref
  135.2 56.5 %all-to-all-done.3 = bf16[512,8,128]{2,1,0:T(8,128)(2,1)S(1)} async-done(((bf16[512,8,128]{2,1,0:T(8,128)(2,1)}), bf16[512,8,128]{2,1,0:T(8,128)(2,1)S(1)}, u32[]{:S(2)}, u32[]{:S(2)}) %all-to-all-start.3) | async-done | bytes 1048608 | tf_op jit(solution)/shard_map/all_to_all | solution.py:254
  191.7 4.1 %sum_rows.1 = f32[2048,256]{1,0:T(8,128)} custom-call(s32[1,2048]{1,0:T(1,128)S(1)} %reshape.52.index_ref, bf16[256,2,8,128]{3,2,1,0:T(8,128)(2,1)S(1)} %bitcast.20), custom_call_target="tpu_custom_call" | custom-call | tf_op jit(solution)/shard_map/sum_rows/pallas_call | solution.py:126
  (3 shorter events, 0.1 us)
Async XLA Ops:
  16.2 29.1 %all-to-all-start.1 = ((s32[32,1,64]{2,1,0:T(1,128)}), s32[32,1,64]{2,1,0:T(1,128)S(1)}, u32[]{:S(2)}, u32[]{:S(2)}) async-start(s32[32,1,64]{2,1,0:T(1,128)} %copy.18), calls=%async_computation.1 | async-start | bytes 32768 | tf_op jit(solution)/shard_map/all_to_all | solution.py:254
  33.6 1.2 copy-start
  45.3 12.7 %copy-start.7 = (s32[256,8]{0,1:T(8,128)S(1)}, s32[256,8]{0,1:T(8,128)}, u32[]{:S(2)}) copy-start(s32[256,8]{0,1:T(8,128)} %param.17) | copy-start | bytes 24580
  45.3 70.5 %copy-start.1 = (bf16[768,256]{1,0:T(8,128)(2,1)S(1)}, bf16[768,256]{1,0:T(8,128)(2,1)}, u32[]{:S(2)}) copy-start(bf16[768,256]{1,0:T(8,128)(2,1)} %first_ref.1) | copy-start | bytes 1179652
  45.3 70.5 %copy-start.2 = (bf16[256,256]{1,0:T(8,128)(2,1)S(1)}, bf16[256,256]{1,0:T(8,128)(2,1)}, u32[]{:S(2)}) copy-start(bf16[256,256]{1,0:T(8,128)(2,1)} %user_ref.1) | copy-start | bytes 393220
  45.3 70.5 %copy-start.3 = (bf16[256,128]{1,0:T(8,128)(2,1)S(1)}, bf16[256,128]{1,0:T(8,128)(2,1)}, u32[]{:S(2)}) copy-start(bf16[256,128]{1,0:T(8,128)(2,1)} %second_ref.1) | copy-start | bytes 196612
  45.3 70.5 %copy-start.4 = (f32[256]{0:T(256)S(1)}, f32[256]{0:T(256)}, u32[]{:S(2)}) copy-start(f32[256]{0:T(256)} %param.12) | copy-start | bytes 3076
  45.3 70.5 %copy-start.5 = (f32[128]{0:T(128)S(1)}, f32[128]{0:T(128)}, u32[]{:S(2)}) copy-start(f32[128]{0:T(128)} %param.14) | copy-start | bytes 1540
  45.4 70.5 %copy-start.6 = (bf16[128]{0:T(256)(128)(2,1)S(1)}, bf16[128]{0:T(256)(128)(2,1)}, u32[]{:S(2)}) copy-start(bf16[128]{0:T(256)(128)(2,1)} %param.15) | copy-start | bytes 772
  48.9 67.0 %all-to-all-start.2 = ((bf16[512,8,128]{2,1,0:T(8,128)(2,1)}), bf16[512,8,128]{2,1,0:T(8,128)(2,1)S(1)}, u32[]{:S(2)}, u32[]{:S(2)}) async-start(bf16[512,8,128]{2,1,0:T(8,128)(2,1)} %bitcast.7), calls=%async_computation.2 | async-start | bytes 2097152 | tf_op jit(solution)/shard_map/all_to_all | solution.py:254
  124.3 67.4 %all-to-all-start.3 = ((bf16[512,8,128]{2,1,0:T(8,128)(2,1)}), bf16[512,8,128]{2,1,0:T(8,128)(2,1)S(1)}, u32[]{:S(2)}, u32[]{:S(2)}) async-start(bf16[512,8,128]{2,1,0:T(8,128)(2,1)} %bitcast.12), calls=%async_computation.3 | async-start | bytes 2097152 | tf_op jit(solution)/shard_map/all_to_all | solution.py:254
